TPU v7x, 512 devices: a whole 4x8x8 slice. The times are simulated.
512 devices in a mesh: dp: 32 (over z, x_hi, core), seq: 16 (over y, x_lo).
Axes of the slice: x: 4 (x_hi: 2, x_lo: 2; x = x_hi * 2 + x_lo), y: 8, z: 8, core: 2. Of those that a mesh axis runs over, the one named last changes fastest.
Arguments:
- features: bfloat16 [32, 2048, 1920], P('dp', 'seq'), may hold values from -48 to 48
- segment_ids: int32 [32, 2048], P('dp'), may hold values from 0 to 7, never falling along the last dimension, each value on 1 to 512 neighbouring positions
- projections: bfloat16 [3, 1920, 1920], P(None, 'seq'), may hold values from -1 to 1
- cotangent: bfloat16 [32, 2048, 1920], P('dp', 'seq'), may hold values from -6 to 6
Outputs:
- context: bfloat16 [32, 2048, 1920], P('dp', 'seq')
- value_grad: float32 [1920, 1920], P('seq')
Inputs may be any that keep to these rules, and one draw needn't show every extreme that they name: `segment_ids`: segment numbers never fall along a sequence; every utterance number appears, each utterance has 1 to 512 frames, and one has exactly 512.
All inputs are finite; a program needn't handle non-finite values.
Results may differ from a plain program's by a relative error of at most 0.011.
Values may be sent and summed in bfloat16 or wider, within the bound.
A program may use at most 64 MiB of HBM per device.

v0:
```python
import jax
import jax.numpy as jnp
from jax import lax
from jax.sharding import PartitionSpec as P

HEAD = 120


def body(features, segment_ids, projections, cotangent):
    frames_local = features[0]
    labels = segment_ids[0]
    local_width = projections.shape[1]
    head_size = HEAD
    local_heads = local_width // head_size
    model_width = frames_local.shape[1]
    weights = projections.reshape(3 * local_width, model_width)
    upstream = lax.all_to_all(cotangent[0], "seq", split_axis=1, concat_axis=0, tiled=True)
    gathered = lax.all_gather(frames_local, "seq", axis=0, tiled=True)
    projected = jnp.einsum(
        "tf,cf->tc", gathered, weights, preferred_element_type=jnp.float32
    ).astype(jnp.bfloat16)
    total_frames = projected.shape[0]
    queries = projected[:, :local_width].reshape(total_frames, local_heads, head_size)
    key_rows = projected[:, local_width : 2 * local_width].reshape(
        total_frames, local_heads, head_size
    )
    values = projected[:, 2 * local_width :].reshape(total_frames, local_heads, head_size)
    upstream_heads = upstream.reshape(total_frames, local_heads, head_size)
    block_rows = min(512, total_frames)
    block_count = total_frames // block_rows
    score_scale = head_size ** (-0.5)

    def weights_of(block_index):
        offset = block_index * block_rows
        query_block = lax.dynamic_slice_in_dim(queries, offset, block_rows, 0)
        row_labels = lax.dynamic_slice_in_dim(labels, offset, block_rows, 0)
        scores = (
            jnp.einsum("qhe,khe->hqk", query_block, key_rows, preferred_element_type=jnp.float32)
            * score_scale
        )
        same_segment = row_labels[:, None] == labels[None, :]
        scores = jnp.where(same_segment[None], scores, -1e30)
        row_max = jnp.max(scores, axis=2, keepdims=True)
        exponent = jnp.exp(scores - row_max)
        attn_weights = (exponent / jnp.sum(exponent, axis=2, keepdims=True)).astype(jnp.bfloat16)
        return (attn_weights, offset)

    def context_of(attn_weights):
        return jnp.einsum(
            "hqk,khe->qhe", attn_weights, values, preferred_element_type=jnp.float32
        ).astype(jnp.bfloat16)

    def value_term(attn_weights, offset):
        grad_block = lax.dynamic_slice_in_dim(upstream_heads, offset, block_rows, 0)
        return jnp.einsum(
            "hqk,qhe->khe", attn_weights, grad_block, preferred_element_type=jnp.float32
        )

    empty_rows = jnp.zeros((total_frames, local_heads, head_size), jnp.float32)

    def joint_step(running, block_index):
        attn_weights, offset = weights_of(block_index)
        return (running + value_term(attn_weights, offset), context_of(attn_weights))

    value_sum, blocks = lax.scan(joint_step, empty_rows, jnp.arange(block_count))
    context = blocks.reshape(total_frames, local_width)
    returned = lax.all_to_all(context, "seq", split_axis=0, concat_axis=1, tiled=True)
    value_rows = value_sum.reshape(total_frames, local_width).astype(jnp.bfloat16)
    partial_grad = jnp.einsum("tw,td->wd", value_rows, gathered, preferred_element_type=jnp.float32)
    summed = lax.psum(partial_grad, "dp")
    value_grad = summed / lax.axis_size("dp")
    return (returned[None], value_grad)


def solution(mesh):
    in_specs = (P("dp", "seq", None), P("dp", None), P(None, "seq", None), P("dp", "seq", None))
    out_specs = (P("dp", "seq", None), P("seq", None))
    return jax.shard_map(body, mesh=mesh, in_specs=in_specs, out_specs=out_specs, check_vma=False)
```

profile of v0, /device:TPU:1, one launch (start us, length us, event | category | flops | bytes accessed | tf_op | source)
XLA Modules:
  0.0 536.6 jit_solution(14925531246365811088)
XLA Ops:
  7.9 2.0 copy.15
  9.9 8.7 %all-to-all-start = ((bf16[128,16,120]{0,2,1:T(8,128)(2,1)}), bf16[128,16,120]{0,2,1:T(8,128)(2,1)S(1)}, u32[]{:S(2)}, u32[]{:S(2)}) async-start(bf16[128,16,120]{0,2,1:T(8,128)(2,1)} %bitcast), calls=%async_computation | async-start | bytes 983040 | tf_op jit(solution)/shard_map/all_to_all | solution.py:17
  18.6 14.4 %all-to-all-done = bf16[128,16,120]{0,2,1:T(8,128)(2,1)S(1)} async-done(((bf16[128,16,120]{0,2,1:T(8,128)(2,1)}), bf16[128,16,120]{0,2,1:T(8,128)(2,1)S(1)}, u32[]{:S(2)}, u32[]{:S(2)}) %all-to-all-start) | async-done | bytes 491552 | tf_op jit(solution)/shard_map/all_to_all | solution.py:17
  34.1 158.1 %all-gather.3.cloned.1.call-done = bf16[1,2048,1920]{2,1,0:T(8,128)(2,1)} async-done(((bf16[1,128,1920]{2,1,0:T(8,128)(2,1)}), bf16[1,2048,1920]{2,1,0:T(8,128)(2,1)}) %all-gather.3.cloned.1.call-update) | async-done | bytes 7864336 | tf_op jit(solution)/shard_map/all_gather | solution.py:18
  192.2 6.5 %fusion.16 = bf16[2048,360]{0,1:T(8,128)(2,1)S(1)} fusion(bf16[360,1920]{1,0:T(8,128)(2,1)S(1)} %bitcast.84, bf16[1,2048,1920]{2,1,0:T(8,128)(2,1)} %all-gather.3.cloned.1.call-done), kind=kOutput, calls=%fused_computation.21 | convolution fusion | flops 2831892480 | bytes 10721280 | tf_op jit(solution)/shard_map/tf,cf->tc/dot_general | solution.py:19
  199.9 36.9 %while.13 = (s32[]{:T(128)}, f32[2048,1,120]{0,2,1:T(8,128)}, bf16[4,512,1,120]{1,3,2,0:T(8,128)(2,1)}, s32[4]{0:T(128)S(1)}, bf16[2048,1,120]{0,2,1:T(8,128)(2,...) while((s32[]{:T(128)}, f32[2048,1,120]{0,2,1:T(8,128)}, ...), condition=%wide.region_3.4_spmd.clone, body=%wide.region_0.3_spmd.clone.sunk | while | flops 764963840 | bytes 24183536 | solution.py:65
  201.3 2.1 fusion.37
  204.8 2.5 fusion.39
  207.3 1.5 fusion.40
  210.2 2.1 fusion.37
  213.8 2.9 fusion.39
  216.6 1.5 fusion.40
  219.5 2.1 fusion.37
  223.1 2.9 fusion.39
  226.0 1.5 fusion.40
  228.8 2.1 fusion.37
  232.4 2.9 fusion.39
  235.3 1.5 fusion.40
  236.7 1.4 copy.17
  239.2 5.3 all-to-all-start.1
  244.6 5.5 %fusion.12 = f32[120,1920]{1,0:T(8,128)} fusion(bf16[1,2048,1920]{2,1,0:T(8,128)(2,1)} %all-gather.3.cloned.1.call-done, f32[2048,1,120]{0,2,1:T(8,128)S(1)} %copy-done.1), kind=kOutput, calls=%fused_computation.17 | convolution fusion | flops 943964160 | bytes 9768960 | tf_op jit(solution)/shard_map/tw,td->wd/dot_general | solution.py:69
  250.1 9.5 %all-to-all-done.1 = bf16[16,128,120]{1,2,0:T(8,128)(2,1)S(1)} async-done(((bf16[16,128,120]{1,2,0:T(8,128)(2,1)}), bf16[16,128,120]{1,2,0:T(8,128)(2,1)S(1)}, u32[]{:S(2)}, u32[]{:S(2)}) %all-to-all-start.1) | async-done | bytes 491552 | tf_op jit(solution)/shard_map/all_to_all | solution.py:67
  260.6 267.0 %all-reduce.2.cloned.1.call-done = f32[120,1920]{1,0:T(8,128)} async-done(((f32[120,1920]{1,0:T(8,128)}), f32[120,1920]{1,0:T(8,128)}) %all-reduce.2.cloned.1.call-update) | async-done | bytes 921616 | tf_op jit(solution)/shard_map/psum | solution.py:70
  527.6 2.2 broadcast_multiply_fusion
  (43 shorter events, 14.0 us)
Async XLA Ops:
  7.2 185.0 %copy-start = (bf16[3,120,1920]{2,1,0:T(8,128)(2,1)S(1)}, bf16[3,120,1920]{2,1,0:T(8,128)(2,1)}, u32[]{:S(2)}) copy-start(bf16[3,120,1920]{2,1,0:T(8,128)(2,1)} %param.8) | copy-start | bytes 4147204
  7.2 185.0 %all-gather.3.cloned.1.call-start = ((), (), s32[]{:S(2)}) async-start(), calls=%async_computation.3 | async-start | bytes 8355840 | tf_op jit(solution)/shard_map/all_gather | solution.py:18
  9.9 23.1 %all-to-all-start = ((bf16[128,16,120]{0,2,1:T(8,128)(2,1)}), bf16[128,16,120]{0,2,1:T(8,128)(2,1)S(1)}, u32[]{:S(2)}, u32[]{:S(2)}) async-start(bf16[128,16,120]{0,2,1:T(8,128)(2,1)} %bitcast), calls=%async_computation | async-start | bytes 983040 | tf_op jit(solution)/shard_map/all_to_all | solution.py:17
  192.2 7.7 %copy-start.3 = (s32[1,2048]{1,0:T(1,128)S(1)}, s32[1,2048]{1,0:T(1,128)}, u32[]{:S(2)}) copy-start(s32[1,2048]{1,0:T(1,128)} %param.7) | copy-start | bytes 24580
  204.8 2.5 copy-start.2
  213.8 2.9 copy-start.2
  223.1 2.9 copy-start.2
  232.4 2.9 copy-start.2
  236.7 7.9 %copy-start.1 = (f32[2048,1,120]{0,2,1:T(8,128)S(1)}, f32[2048,1,120]{0,2,1:T(8,128)}, u32[]{:S(2)}) copy-start(f32[2048,1,120]{0,2,1:T(8,128)} %get-tuple-element.56) | copy-start | bytes 2949124
  239.2 20.3 %all-to-all-start.1 = ((bf16[16,128,120]{1,2,0:T(8,128)(2,1)}), bf16[16,128,120]{1,2,0:T(8,128)(2,1)S(1)}, u32[]{:S(2)}, u32[]{:S(2)}) async-start(bf16[16,128,120]{1,2,0:T(8,128)(2,1)} %copy.18), calls=%async_computation.1 | async-start | bytes 983040 | tf_op jit(solution)/shard_map/all_to_all | solution.py:67
  244.6 283.0 %all-reduce.2.cloned.1.call-start = ((), (), s32[]{:S(2)}) async-start(), calls=%async_computation.2 | async-start | bytes 1843200 | tf_op jit(solution)/shard_map/psum | solution.py:70
Sparse Core Ops, SparseCore 0:
  10.1 182.0 all-gather.2
  250.2 277.2 all-reduce.1
where the time goes:
time: 537 us
  waiting for transfers between devices  450 us (84%)
  matrix products  37.2 us (7%)
  starting transfers between devices  14.1 us (3%)
  between operations  14.1 us (3%)
  local copies, waits for them, and re-layouts  10.7 us (2%)
  other arithmetic  8.07 us (2%)
    psum x1, waiting for transfers between devices, body(): summed = lax.psum(partial_grad, 'dp')  267 us
    all_gather x1, waiting for transfers between devices, body(): gathered = lax.all_gather(frames_local, 'seq', axis=0, tiled=True)  158 us
    all_to_all x1, waiting for transfers between devices, body(): lax.all_to_all(cotangent[0], 'seq', split_axis=1, concat_axis=0, tiled=True)  14.4 us
    dot_general x4, matrix products, value_term(): jnp.einsum('hqk,qhe->khe', attn_weights, grad_block, preferred_element_ty...  11.1 us
  transfers between devices with their start and end apart: 4, of which 4 were waited for; matrix products, arithmetic and copies ran while one was open for 2% of the time, Pallas kernels for 0%

commit v1 on v0

--- a/solution.py
+++ b/solution.py
@@ -67,7 +67,7 @@
     returned = lax.all_to_all(context, "seq", split_axis=0, concat_axis=1, tiled=True)
     value_rows = value_sum.reshape(total_frames, local_width).astype(jnp.bfloat16)
     partial_grad = jnp.einsum("tw,td->wd", value_rows, gathered, preferred_element_type=jnp.float32)
-    summed = lax.psum(partial_grad, "dp")
+    summed = jnp.sum(lax.all_gather(partial_grad, "dp"), axis=0)
     value_grad = summed / lax.axis_size("dp")
     return (returned[None], value_grad)
 

time: 537 us -> 466 us (0.87)
  waiting for transfers between devices: 450 us -> 366 us
  blocking collectives: 0 us -> 20.1 us
  other arithmetic: 8.07 us -> 18 us
  matrix products: 37.2 us -> 28.6 us
    psum x1 -> x0, waiting for transfers between devices: 267 us -> none  [body(): summed = lax.psum(partial_grad, 'dp')]
    all_gather x0 -> x1, waiting for transfers between devices: none -> 193 us  [body(): summed = jnp.sum(lax.all_gather(partial_grad, 'dp'), axis=0)]
    all_to_all x0 -> x1, blocking collectives: none -> 20.1 us  [body(): lax.all_to_all(context, 'seq', split_axis=0, concat_axis=1, tiled=True)]
    reduce_sum x0 -> x1, other arithmetic: none -> 11.1 us  [body(): summed = jnp.sum(lax.all_gather(partial_grad, 'dp'), axis=0)]
    all_to_all x1 -> x0, waiting for transfers between devices: 9.45 us -> none  [body(): lax.all_to_all(context, 'seq', split_axis=0, concat_axis=1, tiled=True)]
    dot_general x4, matrix products: 11.1 us -> 2.36 us  [value_term(): jnp.einsum('hqk,qhe->khe', attn_weights, grad_block, preferred_element_ty...]
  transfers between devices with their start and end apart: 4 -> 3, of which waited for: 4 -> 3; matrix products, arithmetic and copies ran while one was open for 2% -> 1% of each run, Pallas kernels for 0% -> 0%
where the time goes in v1:
time: 466 us
  waiting for transfers between devices  366 us (79%)
  matrix products  28.6 us (6%)
  blocking collectives  20.1 us (4%)
  other arithmetic  18 us (4%)
  between operations  14.1 us (3%)
  starting transfers between devices  8.75 us (2%)
  local copies, waits for them, and re-layouts  7.52 us (2%)
    all_gather x1, waiting for transfers between devices, body(): summed = jnp.sum(lax.all_gather(partial_grad, 'dp'), axis=0)  193 us
    all_gather x1, waiting for transfers between devices, body(): gathered = lax.all_gather(frames_local, 'seq', axis=0, tiled=True)  159 us
    all_to_all x1, blocking collectives, body(): lax.all_to_all(context, 'seq', split_axis=0, concat_axis=1, tiled=True)  20.1 us
    all_to_all x1, waiting for transfers between devices, body(): lax.all_to_all(cotangent[0], 'seq', split_axis=1, concat_axis=0, tiled=True)  14.4 us
    reduce_sum x1, other arithmetic, body(): summed = jnp.sum(lax.all_gather(partial_grad, 'dp'), axis=0)  11.1 us
  transfers between devices with their start and end apart: 3, of which 3 were waited for; matrix products, arithmetic and copies ran while one was open for 1% of the time, Pallas kernels for 0%

profile of v1, /device:TPU:1, one launch (start us, length us, event | category | flops | bytes accessed | tf_op | source)
XLA Modules:
  0.0 465.9 jit_solution(2555591632443291130)
XLA Ops:
  7.9 2.0 copy.15
  9.9 8.7 %all-to-all-start = ((bf16[128,16,120]{0,2,1:T(8,128)(2,1)}), bf16[128,16,120]{0,2,1:T(8,128)(2,1)S(1)}, u32[]{:S(2)}, u32[]{:S(2)}) async-start(bf16[128,16,120]{0,2,1:T(8,128)(2,1)} %bitcast), calls=%async_computation | async-start | bytes 983040 | tf_op jit(solution)/shard_map/all_to_all | solution.py:17
  18.7 14.4 %all-to-all-done = bf16[128,16,120]{0,2,1:T(8,128)(2,1)S(1)} async-done(((bf16[128,16,120]{0,2,1:T(8,128)(2,1)}), bf16[128,16,120]{0,2,1:T(8,128)(2,1)S(1)}, u32[]{:S(2)}, u32[]{:S(2)}) %all-to-all-start) | async-done | bytes 491552 | tf_op jit(solution)/shard_map/all_to_all | solution.py:17
  33.3 158.8 %all-gather.5.cloned.1.call-done = bf16[1,2048,1920]{2,1,0:T(8,128)(2,1)} async-done(((bf16[1,128,1920]{2,1,0:T(8,128)(2,1)}), bf16[1,2048,1920]{2,1,0:T(8,128)(2,1)}) %all-gather.5.cloned.1.call-update) | async-done | bytes 7864336 | tf_op jit(solution)/shard_map/all_gather | solution.py:18
  192.2 6.5 %fusion.16 = bf16[2048,360]{0,1:T(8,128)(2,1)S(1)} fusion(bf16[360,1920]{1,0:T(8,128)(2,1)S(1)} %bitcast.85, bf16[1,2048,1920]{2,1,0:T(8,128)(2,1)} %all-gather.5.cloned.1.call-done), kind=kOutput, calls=%fused_computation.21 | convolution fusion | flops 2831892480 | bytes 10721280 | tf_op jit(solution)/shard_map/tf,cf->tc/dot_general | solution.py:19
  198.7 1.1 slice_bitcast_fusion
  199.8 27.3 %while.13 = (s32[]{:T(128)}, f32[2048,1,120]{0,2,1:T(8,128)S(1)}, bf16[4,512,1,120]{1,3,2,0:T(8,128)(2,1)}, s32[4]{0:T(128)S(1)}, bf16[2048,1,120]{0,2,1:T(8,128...) while((s32[]{:T(128)}, f32[2048,1,120]{0,2,1:T(8,128)S(1)}, ...), condition=%wide.region_3.4_spmd.clone, body=%wide.region_0.3_spmd.clone.sunk | while | flops 764963840 | bytes 22216928 | solution.py:65
  201.0 2.1 fusion.37
  203.7 0.8 divide_convert_fusion.2
  204.5 1.5 fusion.40
  207.8 2.1 fusion.37
  211.4 1.5 fusion.40
  214.6 2.1 fusion.37
  217.4 0.8 divide_convert_fusion.2
  218.2 1.5 fusion.40
  221.5 2.1 fusion.37
  224.2 0.8 divide_convert_fusion.2
  225.0 1.5 fusion.40
  227.1 5.5 %fusion.12 = f32[120,1920]{1,0:T(8,128)} fusion(bf16[1,2048,1920]{2,1,0:T(8,128)(2,1)} %all-gather.5.cloned.1.call-done, f32[2048,1,120]{0,2,1:T(8,128)S(1)} %get-tuple-element.56), kind=kOutput, calls=%fused_computation.17 | convolution fusion | flops 943964160 | bytes 9768960 | tf_op jit(solution)/shard_map/tw,td->wd/dot_general | solution.py:69
  233.3 20.1 %all_to_all.32 = bf16[16,128,120]{1,2,0:T(8,128)(2,1)S(1)} all-to-all(bf16[16,128,120]{1,2,0:T(8,128)(2,1)S(1)} %copy.18), channel_id=1, replica_groups=mesh['dp'=32,'seq'=16] {'seq'}, dimensions={0} | all-to-all | bytes 983040 | tf_op jit(solution)/shard_map/all_to_all | solution.py:67
  253.4 1.0 copy.19
  254.4 192.5 %all-gather.7.cloned.1.call-done = f32[3840,1920]{1,0:T(8,128)} async-done(((f32[120,1920]{1,0:T(8,128)}), f32[3840,1920]{1,0:T(8,128)}) %all-gather.7.cloned.1.call-update) | async-done | bytes 29491216 | tf_op jit(solution)/shard_map/all_gather | solution.py:70
  446.9 11.1 %reduce_sum.18 = f32[120,1920]{1,0:T(8,128)S(1)} reduce(f32[32,120,1920]{2,1,0:T(8,128)} %bitcast.86, f32[]{:T(128)} %constant.23.clone.1), dimensions={0}, to_apply=%region_4.5 | reduce | flops 7142400 | bytes 30412804 | tf_op jit(solution)/shard_map/reduce_sum | solution.py:70
  458.1 1.0 broadcast_multiply_fusion
  (35 shorter events, 10.1 us)
Async XLA Ops:
  7.2 185.0 %copy-start = (bf16[3,120,1920]{2,1,0:T(8,128)(2,1)S(1)}, bf16[3,120,1920]{2,1,0:T(8,128)(2,1)}, u32[]{:S(2)}) copy-start(bf16[3,120,1920]{2,1,0:T(8,128)(2,1)} %param.8) | copy-start | bytes 4147204
  7.2 185.0 %all-gather.5.cloned.1.call-start = ((), (), s32[]{:S(2)}) async-start(), calls=%async_computation.2 | async-start | bytes 8355840 | tf_op jit(solution)/shard_map/all_gather | solution.py:18
  9.9 23.1 %all-to-all-start = ((bf16[128,16,120]{0,2,1:T(8,128)(2,1)}), bf16[128,16,120]{0,2,1:T(8,128)(2,1)S(1)}, u32[]{:S(2)}, u32[]{:S(2)}) async-start(bf16[128,16,120]{0,2,1:T(8,128)(2,1)} %bitcast), calls=%async_computation | async-start | bytes 983040 | tf_op jit(solution)/shard_map/all_to_all | solution.py:17
  18.6 428.3 %all-gather.7.cloned.1.call-start = ((), (), s32[]{:S(2)}) async-start(), calls=%async_computation.3 | async-start | bytes 30412800 | tf_op jit(solution)/shard_map/all_gather | solution.py:70
  192.2 7.6 %copy-start.2 = (s32[1,2048]{1,0:T(1,128)S(1)}, s32[1,2048]{1,0:T(1,128)}, u32[]{:S(2)}) copy-start(s32[1,2048]{1,0:T(1,128)} %param.7) | copy-start | bytes 24580
  227.1 5.6 %copy-start.1 = (bf16[4,512,1,120]{1,3,2,0:T(8,128)(2,1)S(1)}, bf16[4,512,1,120]{1,3,2,0:T(8,128)(2,1)}, u32[]{:S(2)}) copy-start(bf16[4,512,1,120]{1,3,2,0:T(8,128)(2,1)} %get-tuple-element.55) | copy-start | bytes 1474564
Sparse Core Ops, SparseCore 0:
  10.1 182.0 all-gather.4
  232.8 214.1 all-gather.6

commit v2 on v0

--- a/solution.py
+++ b/solution.py
@@ -15,7 +15,9 @@
     model_width = frames_local.shape[1]
     weights = projections.reshape(3 * local_width, model_width)
     upstream = lax.all_to_all(cotangent[0], "seq", split_axis=1, concat_axis=0, tiled=True)
-    gathered = lax.all_gather(frames_local, "seq", axis=0, tiled=True)
+    gathered = jnp.concatenate(
+        lax.all_to_all(jnp.stack([frames_local] * lax.axis_size("seq")), "seq", 0, 0), axis=0
+    )
     projected = jnp.einsum(
         "tf,cf->tc", gathered, weights, preferred_element_type=jnp.float32
     ).astype(jnp.bfloat16)

time: 537 us -> 567 us (1.056)
  blocking collectives: 0 us -> 23.5 us
    all_to_all x1, waiting for transfers between devices: 14.4 us -> 178 us  [body(): lax.all_to_all(jnp.stack([frames_local] * lax.axis_size('seq')), 'seq', 0...]
    all_gather x1 -> x0, waiting for transfers between devices: 158 us -> none  [body(): gathered = lax.all_gather(frames_local, 'seq', axis=0, tiled=True)]
    all_to_all x0 -> x1, blocking collectives: none -> 23.5 us  [body(): lax.all_to_all(cotangent[0], 'seq', split_axis=1, concat_axis=0, tiled=True)]
  transfers between devices with their start and end apart: 4 -> 3, of which waited for: 4 -> 3; matrix products, arithmetic and copies ran while one was open for 2% -> 1% of each run, Pallas kernels for 0% -> 0%
where the time goes in v2:
time: 567 us; the launch traced here: 566 us
  waiting for transfers between devices  455 us (80%)
  matrix products  36.8 us (6%)
  blocking collectives  23.5 us (4%)
  local copies, waits for them, and re-layouts  15.2 us (3%)
  between operations  14.1 us (2%)
  starting transfers between devices  10.4 us (2%)
  other arithmetic  8.07 us (1%)
    psum x1, waiting for transfers between devices, body(): summed = lax.psum(partial_grad, 'dp')  269 us
    all_to_all x1, waiting for transfers between devices, body(): lax.all_to_all(jnp.stack([frames_local] * lax.axis_size('seq')), 'seq', 0...  178 us
    all_to_all x1, blocking collectives, body(): lax.all_to_all(cotangent[0], 'seq', split_axis=1, concat_axis=0, tiled=True)  23.5 us
  transfers between devices with their start and end apart: 3, of which 3 were waited for; matrix products, arithmetic and copies ran while one was open for 1% of the time, Pallas kernels for 0%

profile of v2, /device:TPU:1, one launch (start us, length us, event | category | flops | bytes accessed | tf_op | source)
XLA Modules:
  0.0 566.0 jit_solution(11994227106076140526)
XLA Ops:
  7.2 1.4 copy.15
  8.6 23.5 %all_to_all.37 = bf16[128,16,120]{0,2,1:T(8,128)(2,1)S(1)} all-to-all(bf16[128,16,120]{0,2,1:T(8,128)(2,1)S(1)} %bitcast.84), channel_id=1, replica_groups=mesh['dp'=32,'seq'=16] {'seq'}, dimensions={1} | all-to-all | bytes 983040 | tf_op jit(solution)/shard_map/all_to_all | solution.py:17
  32.1 5.2 stack.3
  37.4 4.7 all-to-all-start.1
  43.2 177.8 %all-to-all-done.1 = bf16[16,128,1920]{2,1,0:T(8,128)(2,1)} async-done(((bf16[16,128,1920]{2,1,0:T(8,128)(2,1)}), bf16[16,128,1920]{2,1,0:T(8,128)(2,1)}, u32[]{:S(2)}, u32[]{:S(2)}) %all-to-all-start.1) | async-done | bytes 7864352 | tf_op jit(solution)/shard_map/all_to_all | solution.py:19
  221.0 6.5 %convolution_convert_fusion.1 = bf16[2048,360]{0,1:T(8,128)(2,1)S(1)} fusion(bf16[2048,1920]{1,0:T(8,128)(2,1)} %bitcast.4, bf16[360,1920]{1,0:T(8,128)(2,1)S(1)} %bitcast.81), kind=kOutput, calls=%fused_computation.17 | convolution fusion | flops 2831892480 | bytes 10721280 | tf_op jit(solution)/shard_map/tf,cf->tc/dot_general | solution.py:21
  228.7 36.3 %while.13 = (s32[]{:T(128)}, f32[2048,1,120]{0,2,1:T(8,128)}, bf16[4,512,1,120]{1,3,2,0:T(8,128)(2,1)}, s32[4]{0:T(128)S(1)}, bf16[2048,1,120]{0,2,1:T(8,128)(2,...) while((s32[]{:T(128)}, f32[2048,1,120]{0,2,1:T(8,128)}, ...), condition=%wide.region_3.4_spmd.clone, body=%wide.region_0.3_spmd.clone.sunk | while | flops 764963840 | bytes 24183536 | solution.py:67
  230.0 2.1 fusion.33
  233.6 2.4 fusion.35
  236.0 1.5 fusion.36
  238.8 2.1 fusion.33
  242.4 2.8 fusion.35
  245.2 1.5 fusion.36
  248.0 2.1 fusion.33
  251.6 2.8 fusion.35
  254.3 1.5 fusion.36
  257.2 2.1 fusion.33
  260.7 2.8 fusion.35
  263.5 1.5 fusion.36
  267.4 5.6 all-to-all-start.2
  273.1 5.5 fusion.12
  278.6 8.8 %all-to-all-done.2 = bf16[16,128,120]{1,2,0:T(8,128)(2,1)S(1)} async-done(((bf16[16,128,120]{1,2,0:T(8,128)(2,1)}), bf16[16,128,120]{1,2,0:T(8,128)(2,1)S(1)}, u32[]{:S(2)}, u32[]{:S(2)}) %all-to-all-start.2) | async-done | bytes 491552 | tf_op jit(solution)/shard_map/all_to_all | solution.py:69
  288.4 268.6 %all-reduce.2.cloned.1.call-done = f32[120,1920]{1,0:T(8,128)} async-done(((f32[120,1920]{1,0:T(8,128)}), f32[120,1920]{1,0:T(8,128)}) %all-reduce.2.cloned.1.call-update) | async-done | bytes 921616 | tf_op jit(solution)/shard_map/psum | solution.py:72
  557.0 2.2 broadcast_multiply_fusion
  (42 shorter events, 14.6 us)
Async XLA Ops:
  7.2 213.8 %copy-start = (bf16[3,120,1920]{2,1,0:T(8,128)(2,1)S(1)}, bf16[3,120,1920]{2,1,0:T(8,128)(2,1)}, u32[]{:S(2)}) copy-start(bf16[3,120,1920]{2,1,0:T(8,128)(2,1)} %param.8) | copy-start | bytes 4147204
  37.4 183.6 %all-to-all-start.1 = ((bf16[16,128,1920]{2,1,0:T(8,128)(2,1)}), bf16[16,128,1920]{2,1,0:T(8,128)(2,1)}, u32[]{:S(2)}, u32[]{:S(2)}) async-start(bf16[16,128,1920]{2,1,0:T(8,128)(2,1)} %stack.3), calls=%async_computation.1 | async-start | bytes 15728640 | tf_op jit(solution)/shard_map/all_to_all | solution.py:19
  221.0 7.7 %copy-start.3 = (s32[1,2048]{1,0:T(1,128)S(1)}, s32[1,2048]{1,0:T(1,128)}, u32[]{:S(2)}) copy-start(s32[1,2048]{1,0:T(1,128)} %param.7) | copy-start | bytes 24580
  233.6 2.4 copy-start.2
  242.4 2.8 copy-start.2
  251.6 2.8 copy-start.2
  260.7 2.8 copy-start.2
  265.0 8.2 %copy-start.1 = (f32[2048,1,120]{0,2,1:T(8,128)S(1)}, f32[2048,1,120]{0,2,1:T(8,128)}, u32[]{:S(2)}) copy-start(f32[2048,1,120]{0,2,1:T(8,128)} %get-tuple-element.56) | copy-start | bytes 2949124
  267.4 19.9 %all-to-all-start.2 = ((bf16[16,128,120]{1,2,0:T(8,128)(2,1)}), bf16[16,128,120]{1,2,0:T(8,128)(2,1)S(1)}, u32[]{:S(2)}, u32[]{:S(2)}) async-start(bf16[16,128,120]{1,2,0:T(8,128)(2,1)} %copy.18), calls=%async_computation.2 | async-start | bytes 983040 | tf_op jit(solution)/shard_map/all_to_all | solution.py:69
  273.1 283.9 %all-reduce.2.cloned.1.call-start = ((), (), s32[]{:S(2)}) async-start(), calls=%async_computation.3 | async-start | bytes 1843200 | tf_op jit(solution)/shard_map/psum | solution.py:72
Sparse Core Ops, SparseCore 0:
  278.7 278.2 all-reduce.1
